TPU v7x, 32 devices: a whole 2x2x4 slice. The times are simulated.
32 devices in a mesh: dp: 8 (over z, y), mp: 4 (over x, core).
Axes of the slice: x: 2, y: 2, z: 4, core: 2. Of those that a mesh axis runs over, the one named last changes fastest.
Arguments:
- grad_parts: bfloat16 [8, 4, 1024, 1024], P('dp', 'mp'), may hold values from -10 to 10
- left_stat: float32 [4, 1024, 1024], P('mp', 'dp'), may hold values from -60 to 500, as said below
- right_stat: float32 [4, 1024, 1024], P('mp', 'dp'), may hold values from -60 to 500, as said below
- left_root: bfloat16 [4, 1024, 1024], P('mp', 'dp'), may hold values from -2 to 2
- right_root: bfloat16 [4, 1024, 1024], P('mp', 'dp'), may hold values from -2 to 2
- due: int32 [4, 2], P('mp'), may hold values 0 or 1
Outputs:
- update: bfloat16 [4, 1024, 1024], P('mp')
- left_new: float32 [4, 1024, 1024], P('mp', 'dp')
- right_new: float32 [4, 1024, 1024], P('mp', 'dp')
- left_out: bfloat16 [4, 1024, 1024], P('mp', 'dp')
- right_out: bfloat16 [4, 1024, 1024], P('mp', 'dp')
Inputs may be any that keep to these rules, and one draw needn't show every extreme that they name: `left_stat`: every block is positive definite. `right_stat`: every block is positive definite. `due`: 1 where that statistic of the block gets a new root in this step.
All inputs are finite; a program needn't handle non-finite values.
Results may differ from a plain program's by a relative error of at most 0.022.
Values may be sent and summed in bfloat16 or wider, within the bound.
A program may use at most 64 MiB of HBM per device.

v0:
```python
import jax
import jax.numpy as jnp
from jax import lax
from jax.sharding import PartitionSpec as P

epsilon = 1e-06
decay = 0.9


def root_batch(whole):
    order_size = whole.shape[-1]
    traces = jnp.trace(whole, axis1=1, axis2=2)
    traces = jnp.where(traces > 0.0, traces, 1.0)
    scale_c = 4.0 * traces / order_size
    identity = jnp.eye(order_size, dtype=jnp.float32)
    initial = ((5.0 * identity[None] - whole / scale_c[:, None, None]) / 4.0).astype(jnp.bfloat16)
    square = jnp.einsum(
        "kij,kjl->kil", initial, initial, preferred_element_type=jnp.float32
    ).astype(jnp.bfloat16)
    fourth = jnp.einsum("kij,kjl->kil", square, square, preferred_element_type=jnp.float32).astype(
        jnp.bfloat16
    )
    combined = (5.0 * initial.astype(jnp.float32) - 4.0 * square.astype(jnp.float32)).astype(
        jnp.bfloat16
    )
    product = jnp.einsum("kij,kjl->kil", fourth, combined, preferred_element_type=jnp.float32)
    return (
        scale_c[:, None, None] ** (-0.25) * (5.0 * initial.astype(jnp.float32) - product) / 4.0
    ).astype(jnp.bfloat16)


def per_device(grad_parts, left_stat, right_stat, left_root, right_root, due):
    partial_value = grad_parts[0]
    grad_rows = lax.psum_scatter(
        partial_value.astype(jnp.float32).astype(jnp.bfloat16),
        "dp",
        scatter_dimension=1,
        tiled=True,
    )
    local_blocks = grad_rows.shape[0]
    row_count = grad_rows.shape[1]
    order_size = grad_rows.shape[2]
    square_sum = jnp.sum(grad_rows.astype(jnp.float32) ** 2)
    grand_sum = lax.psum(square_sum, ("dp", "mp"))
    entry_count = float(lax.axis_size("mp") * local_blocks * order_size * order_size)
    factor = 1.0 / jnp.sqrt(grand_sum / entry_count + epsilon)
    full_grad = lax.all_gather(grad_rows, "dp", axis=1, tiled=True)
    row_start = lax.axis_index("dp") * row_count
    own_cols = lax.dynamic_slice_in_dim(full_grad, row_start, row_count, 2)
    left_prod = jnp.einsum("brk,bck->brc", grad_rows, full_grad, preferred_element_type=jnp.float32)
    right_prod = jnp.einsum("bkr,bkc->brc", own_cols, full_grad, preferred_element_type=jnp.float32)
    left_new = left_stat * decay + left_prod * ((1.0 - decay) / order_size)
    right_new = right_stat * decay + right_prod * ((1.0 - decay) / order_size)
    statistics = jnp.concatenate([left_new, right_new], 0)
    stat_count = statistics.shape[0]
    peer_count = lax.axis_size("dp")
    padding = jnp.zeros((peer_count - stat_count, row_count, order_size), jnp.float32)
    send_slots = jnp.concatenate([statistics, padding], 0)[:, None]
    computed = root_batch(
        lax.all_to_all(send_slots, "dp", split_axis=0, concat_axis=2, tiled=True)[0]
    )[None]
    returned = lax.all_to_all(computed, "dp", split_axis=2, concat_axis=0, tiled=True)
    new_roots = returned[:stat_count, 0]
    due_flags = due.T.reshape(-1)
    old_roots = jnp.concatenate([left_root, right_root], 0)
    roots_used = jnp.where(due_flags[:, None, None] == 1, new_roots, old_roots)
    left_out = roots_used[:local_blocks]
    right_out = roots_used[local_blocks:]
    x_rows = jnp.einsum(
        "brk,bkc->brc", left_out, full_grad, preferred_element_type=jnp.float32
    ).astype(jnp.bfloat16)
    blank = jnp.zeros((local_blocks, row_count, order_size), jnp.float32)
    shard_piece = lax.all_gather(right_out, "dp", axis=1, tiled=True)
    columns = lax.slice_in_dim(x_rows, 0, shard_piece.shape[1], axis=2)
    right_terms = blank + jnp.einsum(
        "brk,bkc->brc", columns, shard_piece, preferred_element_type=jnp.float32
    )
    update_part = (right_terms * factor).astype(jnp.bfloat16)
    update = lax.all_gather(update_part, "dp", axis=1, tiled=True)
    return (update, left_new, right_new, left_out, right_out)


def solution(mesh):
    placed = (
        P("dp", "mp", None, None),
        P("mp", "dp", None),
        P("mp", "dp", None),
        P("mp", "dp", None),
        P("mp", "dp", None),
        P("mp", None),
    )
    return jax.shard_map(
        per_device,
        mesh=mesh,
        in_specs=placed,
        out_specs=(
            P("mp", None, None),
            P("mp", "dp", None),
            P("mp", "dp", None),
            P("mp", "dp", None),
            P("mp", "dp", None),
        ),
        check_vma=False,
    )
```

profile of v0, /device:TPU:0, one launch (start us, length us, event | category | flops | bytes accessed | tf_op | source)
XLA Modules:
  0.0 459.6 jit_solution(12357690563850378942)
XLA Ops:
  7.2 0.0 reduce-scatter.2.cloned.1.call-start
  7.2 0.7 reduce-scatter.2.cloned.1.call-update
  7.9 0.0 all-gather.5.cloned.1.call-start
  7.9 75.1 %reduce-scatter.2.cloned.1.call-done = bf16[1,128,1024]{2,1,0:T(8,128)(2,1)} async-done(((bf16[1,1024,1024]{2,1,0:T(8,128)(2,1)}), bf16[1,128,1024]{2,1,0:T(8,128)(2,1)}) %reduce-scatter.2.cloned.1.call-update) | async-done | bytes 262160 | tf_op jit(solution)/shard_map/reduce_scatter | solution.py:34
  83.0 0.0 all-gather.5.cloned.1.call-update
  83.1 0.1 pad.4.clone
  83.1 50.2 %all-gather.5.cloned.1.call-done = bf16[1,1024,1024]{2,1,0:T(8,128)(2,1)} async-done(((bf16[1,128,1024]{2,1,0:T(8,128)(2,1)}), bf16[1,1024,1024]{2,1,0:T(8,128)(2,1)}) %all-gather.5.cloned.1.call-update) | async-done | bytes 2097168 | tf_op jit(solution)/shard_map/all_gather | solution.py:47
  133.3 0.0 copy-start
  133.3 2.7 fusion.35
  136.0 0.0 copy-done
  136.1 0.0 copy-start.2
  136.1 1.7 fusion.32
  137.8 0.0 copy-start.3
  137.8 2.5 maximum_bitcast_fusion
  140.3 0.0 copy-done.2
  140.3 0.0 copy-done.3
  140.3 4.5 all-to-all-start
  144.8 92.3 %all-to-all-done = f32[8,1,128,1024]{3,2,1,0:T(8,128)} async-done(((f32[8,1,128,1024]{3,2,1,0:T(8,128)}), f32[8,1,128,1024]{3,2,1,0:T(8,128)}, u32[]{:S(2)}, u32[]{:S(2)}) %all-to-all-start) | async-done | bytes 4194336 | tf_op jit(solution)/shard_map/all_to_all | solution.py:60
  237.1 2.9 select_reduce_fusion
  241.4 2.7 multiply_convert_fusion.1
  244.1 3.7 convolution_convert_fusion
  247.8 1.9 fusion.1
  249.7 10.1 %fusion.14 = bf16[1,1,1024,1024]{3,2,1,0:T(8,128)(2,1)} fusion(bf16[1024,1024]{1,0:T(8,128)(2,1)} %convolution_convert_fusion, bf16[1024,1024]{1,0:T(8,128)(2,1)} %fusion.1, f32[]{:T(128)} %bitcast.9), kind=kOutput, calls=%fused_computation.26 | convolution fusion | flops 4308598784 | bytes 6291460 | tf_op jit(solution)/shard_map/kij,kjl->kil/dot_general | solution.py:26
  259.8 6.8 %copy.15 = bf16[1,1,1024,1024]{3,1,0,2:T(2,128)(2,1)} copy(bf16[1,1,1024,1024]{3,2,1,0:T(8,128)(2,1)} %fusion.14) | data formatting | bytes 4194304 | tf_op jit(solution)/shard_map/broadcast_in_dim | solution.py:59
  266.5 0.5 broadcast.156
  267.1 14.3 %reduce.1 = bf16[1024,1024]{1,0:T(8,128)(2,1)} reduce(bf16[1024,1,1,1024]{3,2,1,0:T(2,128)(2,1)} %bitcast.79, bf16[]{:T(256)} %broadcast.156), dimensions={1,2}, to_apply=%bitcast.78.reduce_sub_computation | reduce | bytes 4194306
  281.3 0.0 copy-start.7
  281.3 6.3 %reshape.163 = bf16[8,2,65536]{2,1,0:T(2,128)(2,1)} reshape(bf16[1024,1024]{1,0:T(8,128)(2,1)} %reduce.1) | data formatting | bytes 4194304
  287.6 4.4 all-to-all-start.1
  292.0 0.0 all-gather.7.cloned.1.call-start
  292.1 0.0 copy-done.7
  292.1 47.0 %all-to-all-done.1 = bf16[8,2,65536]{2,1,0:T(2,128)(2,1)} async-done(((bf16[8,2,65536]{2,1,0:T(2,128)(2,1)}), bf16[8,2,65536]{2,1,0:T(2,128)(2,1)}, u32[]{:S(2)}, u32[]{:S(2)}) %all-to-all-start.1) | async-done | bytes 2097184 | tf_op jit(solution)/shard_map/all_to_all | solution.py:62
  339.1 6.7 %reshape.164 = bf16[1024,1,1,1024]{3,2,1,0:T(2,128)(2,1)} reshape(bf16[8,2,65536]{2,1,0:T(2,128)(2,1)} %all-to-all-done.1) | data formatting | bytes 4194304
  345.8 0.0 copy-start.5
  345.8 0.0 copy-start.6
  345.8 0.0 copy-start.1
  345.8 3.1 copy.13
  348.9 0.0 copy-done.5
  348.9 0.0 copy-done.6
  348.9 0.1 fusion.48
  349.0 0.7 fusion.57
  349.8 0.0 copy-start.4
  349.8 0.0 all-gather.7.cloned.1.call-update
  349.8 0.0 all-gather.9.cloned.1.call-start
  349.9 0.0 copy-done.1
  349.9 0.7 multiply_reduce_fusion
  350.6 39.5 %psum.7 = f32[]{:T(128)} all-reduce(f32[]{:T(128)} %multiply_reduce_fusion), channel_id=1, replica_groups=mesh['dp'=8,'mp'=4] {'dp','mp'}, use_global_device_ids=true, to_apply=%region_3.4 | all-reduce | flops 1 | bytes 8 | tf_op jit(solution)/shard_map/psum | solution.py:44
  390.8 8.3 %all-gather.7.cloned.1.call-done = bf16[1,1024,1024]{2,1,0:T(8,128)(2,1)} async-done(((bf16[1,128,1024]{2,1,0:T(8,128)(2,1)}), bf16[1,1024,1024]{2,1,0:T(8,128)(2,1)}) %all-gather.7.cloned.1.call-update) | async-done | bytes 2097168 | tf_op jit(solution)/shard_map/all_gather | solution.py:73
  399.1 3.1 fusion.41
  402.2 0.0 all-gather.9.cloned.1.call-update
  402.2 47.8 %all-gather.9.cloned.1.call-done = bf16[1024,1024]{1,0:T(8,128)(2,1)} async-done(((bf16[128,1024]{1,0:T(8,128)(2,1)}), bf16[1024,1024]{1,0:T(8,128)(2,1)}) %all-gather.9.cloned.1.call-update) | async-done | bytes 2097168 | tf_op jit(solution)/shard_map/all_gather | solution.py:79
  450.0 3.1 copy.17
  453.1 0.0 copy-done.4
  (3 shorter events, 0.0 us)
Async XLA Ops:
  7.2 75.9 %reduce-scatter.2.cloned.1.call-start = ((), (), s32[]{:S(2)}) async-start(), calls=%async_computation.3 | async-start | bytes 2359296 | tf_op jit(solution)/shard_map/reduce_scatter | solution.py:34
  7.9 125.4 %all-gather.5.cloned.1.call-start = ((), (), s32[]{:S(2)}) async-start(), calls=%async_computation.4 | async-start | bytes 2359296 | tf_op jit(solution)/shard_map/all_gather | solution.py:47
  133.3 2.7 copy-start
  136.1 4.2 copy-start.2
  137.8 2.5 copy-start.3
  140.3 96.8 %all-to-all-start = ((f32[8,1,128,1024]{3,2,1,0:T(8,128)}), f32[8,1,128,1024]{3,2,1,0:T(8,128)}, u32[]{:S(2)}, u32[]{:S(2)}) async-start(f32[8,1,128,1024]{3,2,1,0:T(8,128)} %maximum_bitcast_fusion), calls=%async_computation.1 | async-start | bytes 8388608 | tf_op jit(solution)/shard_map/all_to_all | solution.py:60
  281.3 10.7 %copy-start.7 = (s32[1,2]{1,0:T(1,128)S(1)}, s32[1,2]{1,0:T(1,128)}, u32[]{:S(2)}) copy-start(s32[1,2]{1,0:T(1,128)} %param.11) | copy-start | bytes 28
  287.6 51.4 %all-to-all-start.1 = ((bf16[8,2,65536]{2,1,0:T(2,128)(2,1)}), bf16[8,2,65536]{2,1,0:T(2,128)(2,1)}, u32[]{:S(2)}, u32[]{:S(2)}) async-start(bf16[8,2,65536]{2,1,0:T(2,128)(2,1)} %reshape.163), calls=%async_computation.2 | async-start | bytes 4194304 | tf_op jit(solution)/shard_map/all_to_all | solution.py:62
  292.0 107.1 %all-gather.7.cloned.1.call-start = ((), (), s32[]{:S(2)}) async-start(), calls=%async_computation.5 | async-start | bytes 2359296 | tf_op jit(solution)/shard_map/all_gather | solution.py:73
  345.8 3.1 copy-start.5
  345.8 3.1 copy-start.6
  345.8 4.0 copy-start.1
  349.8 103.3 %copy-start.4 = (bf16[1,128,1024]{2,1,0:T(8,128)(2,1)}, bf16[1,128,1024]{2,1,0:T(8,128)(2,1)S(1)}, u32[]{:S(2)}) copy-start(bf16[1,128,1024]{2,1,0:T(8,128)(2,1)S(1)} %get-tuple-element.17) | copy-start | bytes 786436
  349.8 100.2 %all-gather.9.cloned.1.call-start = ((), (), s32[]{:S(2)}) async-start(), calls=%async_computation.6 | async-start | bytes 2359296 | tf_op jit(solution)/shard_map/all_gather | solution.py:79
Sparse Core Ops, SparseCore 0:
  11.5 71.4 reduce-scatter.1
  85.2 48.0 all-gather.4
  349.9 49.1 all-gather.6
  402.3 47.6 all-gather.8
where the time goes:
time: 460 us
  waiting for transfers between devices  321 us (70%)
  blocking collectives  39.5 us (9%)
  local copies, waits for them, and re-layouts  27.3 us (6%)
  other arithmetic  25.2 us (5%)
  matrix products  21.2 us (5%)
  between operations  15.9 us (3%)
  starting transfers between devices  9.05 us (2%)
    all_to_all x1, waiting for transfers between devices, per_device(): lax.all_to_all(send_slots, 'dp', split_axis=0, concat_axis=2, tiled=True)[0]  92.3 us
    reduce_scatter x1, waiting for transfers between devices, per_device(): lax.psum_scatter(partial_value.astype(jnp.float32).astype(jnp.bfloat16),...  75.1 us
    all_gather x1, waiting for transfers between devices, per_device(): full_grad = lax.all_gather(grad_rows, 'dp', axis=1, tiled=True)  50.2 us
    all_gather x1, waiting for transfers between devices, per_device(): update = lax.all_gather(update_part, 'dp', axis=1, tiled=True)  47.8 us
    all_to_all x1, waiting for transfers between devices, per_device(): lax.all_to_all(computed, 'dp', split_axis=2, concat_axis=0, tiled=True)  47 us
    psum x1, blocking collectives, per_device(): grand_sum = lax.psum(square_sum, ('dp', 'mp'))  39.5 us
    unnamed x21, local copies, waits for them, and re-layouts  19.7 us
    unnamed x1, other arithmetic  14.3 us
  transfers between devices with their start and end apart: 6, of which 6 were waited for; matrix products, arithmetic and copies ran while one was open for 0% of the time, Pallas kernels for 0%

commit v1 on v0

v1 whole, which is shorter than its diff:
```python
import functools

import jax
import jax.numpy as jnp
from jax import lax
from jax.experimental import pallas as pl
from jax.experimental.pallas import tpu as pltpu
from jax.sharding import PartitionSpec as P

epsilon = 1e-06
decay = 0.9
MESH = pl.DeviceIdType.MESH


def exchange(n, m, part_ref, zown_ref, g_ref, z_ref, s_ref, up_buf, dn_buf, y_send, y_got, total, s_buf,
             rs_sem, ys_sem, z_sem, g_sem, zy_sem, gy_sem, s_sem, own_sem):
    outer = n // 2
    rows, cols = total.shape
    me, mp = lax.axis_index("dp"), lax.axis_index("mp")
    z, y = lax.div(me, 2), lax.rem(me, 2)
    other = 1 - y
    up, dn, pair = (me + 2, mp), (me - 2, mp), (2 * z + other, mp)
    has_up, has_dn = z < outer - 1, z > 0
    peers = [(me, lax.rem(mp + d, m)) for d in range(1, m)]

    barrier = pltpu.get_barrier_semaphore()

    def greet(dev):
        pl.semaphore_signal(barrier, inc=1, device_id=dev, device_id_type=MESH)

    for dev in [pair] + peers:
        greet(dev)
    pl.when(has_up)(lambda: greet(up))
    pl.when(has_dn)(lambda: greet(dn))
    pl.semaphore_wait(barrier, m + has_up.astype(jnp.int32) + has_dn.astype(jnp.int32))

    def rc(src, dst, sems, dev):
        return pltpu.make_async_remote_copy(
            src_ref=src, dst_ref=dst, send_sem=sems.at[0], recv_sem=sems.at[1],
            device_id=dev, device_id_type=MESH)

    def at_rows(ref, block):
        return ref.at[..., pl.ds(pl.multiple_of(block * rows, rows), rows), :]

    def mine(a, h):
        return part_ref.at[pl.ds((2 * a + h) * rows, rows), :]

    up_order = [(a, h) for a in range(outer - 1, 0, -1) for h in (0, 1)]
    dn_order = [(a, h) for a in range(outer - 1) for h in (0, 1)]

    def rs_copy(way, a, h, src=None):
        buf, dev = ((up_buf, up), (dn_buf, dn))[way]
        return rc(buf.at[a, h] if src is None else src, buf.at[a, h], rs_sem.at[way, a, h], dev)

    @pl.when(z == 0)
    def _():
        for a, h in up_order:
            rs_copy(0, a, h, mine(a, h)).start()

    @pl.when(z == outer - 1)
    def _():
        for a, h in dn_order:
            rs_copy(1, a, h, mine(a, h)).start()

    class Gather:
        def __init__(self, own, full, sem, sem_y):
            self.own, self.full, self.sem, self.sem_y = own, full, sem, sem_y

        def line(self, way, step, block):
            dev = (up, dn)[way]
            where = at_rows(self.full, 2 * block + y)
            return rc(self.own if step == 0 else where, where, self.sem.at[way, step], dev)

        def across(self, index, block, side):
            where = at_rows(self.full, 2 * block + side)
            return rc(self.own if index == 0 else where, where, self.sem_y.at[index], pair)

        def start(self):
            pl.when(has_up)(lambda: self.line(0, 0, z).start())
            pl.when(has_dn)(lambda: self.line(1, 0, z).start())
            self.across(0, z, y).start()

        def arrival(self, way, step):
            return z - 1 - step if way == 0 else z + 1 + step

        def exists(self, way, step):
            return z - 1 - step >= 0 if way == 0 else z + 1 + step < outer

        def step(self, s):
            for way in (0, 1):
                block = self.arrival(way, s)

                @pl.when(self.exists(way, s))
                def _():
                    self.line(way, s, block).wait_recv()
                    if s + 1 < outer - 1:
                        pl.when((has_up, has_dn)[way])(lambda: self.line(way, s + 1, block).start())
                    self.across(1 + 2 * s + way, block, y).start()

        def finish(self):
            self.across(0, z, other).wait()
            for s in range(outer - 1):
                for way in (0, 1):
                    sent = jnp.logical_and((z - s >= 0, z + s < outer)[way], (has_up, has_dn)[way])
                    pl.when(sent)(lambda: self.line(way, s, z).wait_send())

                    @pl.when(self.exists(way, s))
                    def _():
                        self.across(1 + 2 * s + way, self.arrival(way, s), other).wait()

    zs = Gather(zown_ref, z_ref, z_sem, zy_sem)
    own_z = pltpu.make_async_copy(zown_ref, at_rows(z_ref, me), own_sem)
    zs.start()
    own_z.start()

    def relay(way, a, h):
        rs_copy(way, a, h).wait_recv()
        buf = (up_buf, dn_buf)[way]
        both = buf[a, h].astype(jnp.float32) + mine(a, h)[...].astype(jnp.float32)
        buf[a, h] = both.astype(jnp.bfloat16)
        rs_copy(way, a, h).start()

    for k in range(outer - 1):
        a, b = outer - 1 - k, k

        @pl.when(jnp.logical_and(z > 0, z < a))
        def _():
            for h in (0, 1):
                relay(0, a, h)

        @pl.when(jnp.logical_and(z < outer - 1, z > b))
        def _():
            for h in (0, 1):
                relay(1, b, h)

        zs.step(k)

    def partial_sum(side):
        total[...] = part_ref[pl.ds(pl.multiple_of((2 * z + side) * rows, rows), rows), :].astype(jnp.float32)

        @pl.when(has_dn)
        def _():
            rs_copy(0, z, side).wait_recv()
            total[...] += up_buf[z, side].astype(jnp.float32)

        @pl.when(has_up)
        def _():
            rs_copy(1, z, side).wait_recv()
            total[...] += dn_buf[z, side].astype(jnp.float32)

    partial_sum(other)
    y_send[...] = total[...].astype(jnp.bfloat16)
    cross = rc(y_send, y_got, ys_sem, pair)
    cross.start()
    partial_sum(y)
    cross.wait()
    own_rows = at_rows(g_ref, me)
    own_rows[...] = (total[...] + y_got[...].astype(jnp.float32)).astype(jnp.bfloat16)

    gs = Gather(own_rows, g_ref, g_sem, gy_sem)
    gs.start()
    for k in range(outer - 1):
        gs.step(k)
    gs.finish()

    def square(i, acc):
        v = g_ref[pl.ds(pl.multiple_of(i * rows, rows), rows), :].astype(jnp.float32)
        return acc + jnp.sum((v * v).reshape(rows // 8, 8, cols), axis=0)

    wide = lax.fori_loop(0, n, square, jnp.zeros((8, cols), jnp.float32))
    s_buf[0] = sum(wide[:, i * 128:(i + 1) * 128] for i in range(cols // 128))
    sends = [rc(s_buf.at[0], s_buf.at[d], s_sem.at[d], peers[d - 1]) for d in range(1, m)]
    for c in sends:
        c.start()

    @pl.when(has_up)
    def _():
        for a, h in up_order:
            pl.when(z < a)(lambda: rs_copy(0, a, h).wait_send())

    @pl.when(has_dn)
    def _():
        for a, h in dn_order:
            pl.when(z > a)(lambda: rs_copy(1, a, h).wait_send())

    own_z.wait()
    zs.finish()
    for c in sends:
        c.wait()
    s_ref[0] = s_buf[0]
    s_ref[1] = sum(s_buf[d] for d in range(m))


def gathered(part, z_own):
    n, m = lax.axis_size("dp"), lax.axis_size("mp")
    outer = n // 2
    order, cols = part.shape
    rows = order // n
    bf, f32 = jnp.bfloat16, jnp.float32
    vm = pl.BlockSpec(memory_space=pltpu.VMEM)
    dma = pltpu.SemaphoreType.DMA
    return pl.pallas_call(
        functools.partial(exchange, n, m),
        out_shape=(
            jax.ShapeDtypeStruct((order, cols), bf),
            jax.ShapeDtypeStruct((2, order, cols), bf),
            jax.ShapeDtypeStruct((2, 8, 128), f32),
        ),
        in_specs=[vm, vm],
        out_specs=(vm, vm, vm),
        scratch_shapes=[
            pltpu.VMEM((outer, 2, rows, cols), bf),
            pltpu.VMEM((outer, 2, rows, cols), bf),
            pltpu.VMEM((rows, cols), bf),
            pltpu.VMEM((rows, cols), bf),
            pltpu.VMEM((rows, cols), f32),
            pltpu.VMEM((m, 8, 128), f32),
            dma((2, outer, 2, 2)),
            dma((2,)),
            dma((2, outer - 1, 2)),
            dma((2, outer - 1, 2)),
            dma((2 * outer - 1, 2)),
            dma((2 * outer - 1, 2)),
            dma((m, 2)),
            dma,
        ],
        compiler_params=pltpu.CompilerParams(collective_id=0, has_side_effects=True),
    )(part, z_own)


def dot(a, b, dims):
    return lax.dot_general(a, b, (dims, ((), ())), preferred_element_type=jnp.float32)


def root_of(old, prod, square_sum, due):
    order = old.shape[0]
    bf, f32 = jnp.bfloat16, jnp.float32
    gain = (1.0 - decay) / order
    trace = decay * jnp.trace(old.astype(f32)) + gain * square_sum
    trace = jnp.where(trace > 0.0, trace, 1.0)
    scale_c = 4.0 * trace / order
    eye = jnp.eye(order, dtype=f32)
    stat = old.astype(f32) * decay + prod * gain
    t0 = ((5.0 * eye - stat / scale_c) / 4.0).astype(bf)
    p = dot(t0, t0, ((1,), (0,))).astype(bf)
    q = dot(p, p, ((1,), (0,))).astype(bf)
    w = (5.0 * t0.astype(f32) - 4.0 * p.astype(f32)).astype(bf)
    qw = dot(q, w, ((1,), (0,)))
    root = (scale_c ** (-0.25) * (5.0 * t0.astype(f32) - qw) / 4.0).astype(bf)
    return jnp.where(due == 1, root, old)


def per_device(grad_parts, left_stat, right_stat, left_root, right_root, due):
    bf = jnp.bfloat16
    part = grad_parts[0, 0]
    rows, order = left_stat.shape[1:]
    z_own = jnp.stack([
        jnp.where(due[0, 0] == 1, left_stat[0].astype(bf), left_root[0]),
        jnp.where(due[0, 1] == 1, right_stat[0].astype(bf), right_root[0]),
    ])
    grad, zf, sums = gathered(part, z_own)
    square_sum, grand_sum = jnp.sum(sums[0]), jnp.sum(sums[1])
    entry_count = float(lax.axis_size("mp") * order * order)
    factor = 1.0 / jnp.sqrt(grand_sum / entry_count + epsilon)
    start = lax.axis_index("dp") * rows
    gain = (1.0 - decay) / order
    g_rows = lax.dynamic_slice_in_dim(grad, start, rows, 0)
    g_cols = lax.dynamic_slice_in_dim(grad, start, rows, 1)
    left_new = left_stat * decay + dot(g_rows, grad, ((1,), (1,)))[None] * gain
    right_new = right_stat * decay + dot(g_cols, grad, ((0,), (0,)))[None] * gain
    left = root_of(zf[0], dot(grad, grad, ((1,), (1,))), square_sum, due[0, 0])
    right = root_of(zf[1], dot(grad, grad, ((0,), (0,))), square_sum, due[0, 1])
    x = dot(left, grad, ((1,), (0,))).astype(bf)
    update = (dot(x, right, ((1,), (0,))) * factor).astype(bf)[None]
    left_out = lax.dynamic_slice_in_dim(left, start, rows, 0)[None]
    right_out = lax.dynamic_slice_in_dim(right, start, rows, 0)[None]
    return (update, left_new, right_new, left_out, right_out)


def solution(mesh):
    placed = (
        P("dp", "mp", None, None),
        P("mp", "dp", None),
        P("mp", "dp", None),
        P("mp", "dp", None),
        P("mp", "dp", None),
        P("mp", None),
    )
    return jax.shard_map(
        per_device,
        mesh=mesh,
        in_specs=placed,
        out_specs=(
            P("mp", None, None),
            P("mp", "dp", None),
            P("mp", "dp", None),
            P("mp", "dp", None),
            P("mp", "dp", None),
        ),
        check_vma=False,
    )
```

time: 460 us -> 193 us (0.42)
  waiting for transfers between devices: 321 us -> 0 us
  Pallas kernels: 0 us -> 124 us
  blocking collectives: 39.5 us -> 0 us
  matrix products: 21.2 us -> 49.5 us
  local copies, waits for them, and re-layouts: 27.3 us -> 7.34 us
  other arithmetic: 25.2 us -> 6.62 us
  between operations: 15.9 us -> 4.77 us
  starting transfers between devices: 9.05 us -> 0 us
    all_to_all x2 -> x0, waiting for transfers between devices: 139 us -> none  [the longest x1 92.3 us: per_device(): lax.all_to_all(send_slots, 'dp', split_axis=0, concat_axis=2, tiled=True)[0]]
    pallas_call x0 -> x1, Pallas kernels: none -> 124 us  [gathered(): pl.pallas_call(functools.partial(exchange, n, m), out_shape=(jax.ShapeDty...]
    all_gather x3 -> x0, waiting for transfers between devices: 106 us -> none  [the longest x1 50.2 us: per_device(): full_grad = lax.all_gather(grad_rows, 'dp', axis=1, tiled=True)]
    reduce_scatter x1 -> x0, waiting for transfers between devices: 75.1 us -> none  [per_device(): lax.psum_scatter(partial_value.astype(jnp.float32).astype(jnp.bfloat16),...]
    psum x1 -> x0, blocking collectives: 39.5 us -> none  [per_device(): grand_sum = lax.psum(square_sum, ('dp', 'mp'))]
    dot_general x5 -> x9, matrix products: 21.2 us -> 49.5 us  [dot(): lax.dot_general(a, b, (dims, ((), ())), preferred_element_type=jnp.float32)]
    unnamed x21 -> x10, local copies, waits for them, and re-layouts: 19.7 us -> 2.69 us
    unnamed x1 -> x0, other arithmetic: 14.3 us -> none
  transfers between devices with their start and end apart: 6 -> 0, of which waited for: 6 -> 0; matrix products, arithmetic and copies ran while one was open for 0% -> 0% of each run, Pallas kernels for 0% -> 0%
where the time goes in v1:
time: 193 us
  Pallas kernels  124 us (64%)
  matrix products  49.5 us (26%)
  local copies, waits for them, and re-layouts  7.34 us (4%)
  other arithmetic  6.62 us (3%)
  between operations  4.77 us (2%)
    pallas_call x1, Pallas kernels, gathered(): pl.pallas_call(functools.partial(exchange, n, m), out_shape=(jax.ShapeDty...  124 us
    dot_general x9, matrix products, dot(): lax.dot_general(a, b, (dims, ((), ())), preferred_element_type=jnp.float32)  49.5 us

profile of v1, /device:TPU:0, one launch (start us, length us, event | category | flops | bytes accessed | tf_op | source)
XLA Modules:
  0.0 192.6 jit_solution(7433944834649819103)
XLA Ops:
  0.6 1.3 fusion.44
  3.2 1.4 convert_select_fusion.2
  4.6 0.8 pad_maximum_fusion.zown_ref
  5.5 124.3 %shard_map.101 = (bf16[1024,1024]{1,0:T(8,128)(2,1)}, bf16[2,1024,1024]{2,1,0:T(8,128)(2,1)}, f32[2,8,128]{2,1,0:T(8,128)}) custom-call(bf16[1024,1024]{1,0:T(8,128)(2,1)} %bitcast.42, bf16[2,128,1024]{2,1,0:T(8,128)(2,1)} %pad_maximum_fusion.zown_ref), custom_call_target="tpu_custom_call" | custom-call | tf_op jit(solution)/shard_map/pallas_call | solution.py:202
  129.8 1.3 slice_reduce_fusion.1
  131.8 0.0 copy-start
  131.8 3.1 %fusion = (f32[]{:T(128)}, f32[]{:T(128)}) fusion(bf16[2,1024,1024]{2,1,0:T(8,128)(2,1)} %get-tuple-element.8), kind=kLoop, calls=%fused_computation.6 | loop fusion | flops 7340030 | bytes 4194312 | tf_op jit(solution)/shard_map/jit(trace)/reduce_sum | solution.py:239
  136.2 0.0 copy-done
  136.2 4.7 %fusion.8 = bf16[1024,1024]{1,0:T(8,128)(2,1)S(1)} fusion(bf16[1024,1024]{1,0:T(8,128)(2,1)S(1)} %copy-done, f32[]{:T(128)S(6)} %div.39, bf16[2,1024,1024]{2,1,0:T(8,128)(2,1)} %get-tuple-element.8), kind=kOutput, calls=%fused_computation.22 | convolution fusion | flops 2157969408 | bytes 8388612 | tf_op jit(solution)/shard_map/dot_general | solution.py:232
  140.9 0.0 copy-start.4
  140.9 1.3 copy-done.4
  142.3 3.7 %convolution_convert_fusion = bf16[1024,1024]{1,0:T(8,128)(2,1)} fusion(bf16[1024,1024]{1,0:T(8,128)(2,1)S(1)} %fusion.8), kind=kOutput, calls=%fused_computation.35 | convolution fusion | flops 2148532224 | bytes 4194304 | tf_op jit(solution)/shard_map/dot_general | solution.py:232
  146.0 10.9 %bitcast_select_fusion = bf16[1024,1024]{1,0:T(8,128)(2,1)} fusion(pred[]{:T(512)} %bitcast.2, bf16[2,1024,1024]{2,1,0:T(8,128)(2,1)} %get-tuple-element.8, bf16[1024,1024]{1,0:T(8,128)(2,1)} %convolution_convert_fusion, bf16[1024,1024]{1,0:T(8,128)(2,1)} %copy-done.4, f32[]{:T(128)S(6)} %pow.7), kind=kOutput, calls=%fused_computation.26 | convolution fusion | flops 4309647360 | bytes 14680580 | tf_op jit(solution)/shard_map/dot_general | solution.py:232
  157.6 4.4 %fusion.9 = bf16[1024,1024]{1,0:T(8,128)(2,1)S(1)} fusion(bf16[1024,1024]{1,0:T(8,128)(2,1)S(1)} %copy-done, f32[]{:T(128)S(6)} %div.34, bf16[2,1024,1024]{2,1,0:T(8,128)(2,1)} %get-tuple-element.8), kind=kOutput, calls=%fused_computation.23 | convolution fusion | flops 2157969408 | bytes 8388612 | tf_op jit(solution)/shard_map/dot_general | solution.py:232
  162.0 0.0 copy-start.3
  162.0 1.3 copy-done.3
  163.3 3.8 %convolution_convert_fusion.1 = bf16[1024,1024]{1,0:T(8,128)(2,1)} fusion(bf16[1024,1024]{1,0:T(8,128)(2,1)S(1)} %fusion.9), kind=kOutput, calls=%fused_computation.36 | convolution fusion | flops 2148532224 | bytes 4194304 | tf_op jit(solution)/shard_map/dot_general | solution.py:232
  167.2 11.0 %bitcast_select_fusion.1 = bf16[1024,1024]{1,0:T(8,128)(2,1)} fusion(pred[]{:T(512)} %bitcast, bf16[2,1024,1024]{2,1,0:T(8,128)(2,1)} %get-tuple-element.8, bf16[1024,1024]{1,0:T(8,128)(2,1)} %convolution_convert_fusion.1, bf16[1024,1024]{1,0:T(8,128)(2,1)} %copy-done.3, f32[]{:T(128)S(6)} %pow.6), kind=kOutput, calls=%fused_computation.27 | convolution fusion | flops 4309647360 | bytes 14680580 | tf_op jit(solution)/shard_map/dot_general | solution.py:232
  178.2 0.0 copy-start.1
  178.2 8.1 %fusion.19 = bf16[1,1024,1024]{2,1,0:T(8,128)(2,1)} fusion(f32[]{:T(128)S(6)} %sqrt.3, bf16[1024,1024]{1,0:T(8,128)(2,1)} %bitcast_select_fusion, bf16[1024,1024]{1,0:T(8,128)(2,1)} %bitcast_select_fusion.1, bf16[1024,1024]{1,0:T(8,128)(2,1)S(1)} %copy-done), kind=kOutput, calls=%fused_computation.37 | convolution fusion | flops 4298113024 | bytes 8388612 | tf_op jit(solution)/shard_map/dot_general | solution.py:232
  186.3 0.0 copy-start.2
  186.3 0.0 copy-done.1
  186.3 1.6 fusion.24
  187.9 0.0 copy-done.2
  187.9 1.3 fusion.25
  189.2 1.7 dynamic-slice_bitcast_fusion.1
  190.9 1.7 dynamic-slice_bitcast_fusion
Async XLA Ops:
  131.8 4.4 %copy-start = (bf16[1024,1024]{1,0:T(8,128)(2,1)S(1)}, bf16[1024,1024]{1,0:T(8,128)(2,1)}, u32[]{:S(2)}) copy-start(bf16[1024,1024]{1,0:T(8,128)(2,1)} %get-tuple-element.10) | copy-start | bytes 6291460
  140.9 1.3 copy-start.4
  162.0 1.3 copy-start.3
  178.2 8.1 %copy-start.1 = (f32[1,128,1024]{2,1,0:T(8,128)S(1)}, f32[1,128,1024]{2,1,0:T(8,128)}, u32[]{:S(2)}) copy-start(f32[1,128,1024]{2,1,0:T(8,128)} %param.7) | copy-start | bytes 1572868
  186.3 1.6 copy-start.2

commit v2 on v1

--- a/solution.py
+++ b/solution.py
@@ -12,8 +12,11 @@
 MESH = pl.DeviceIdType.MESH
 
 
-def exchange(n, m, part_ref, zown_ref, g_ref, z_ref, s_ref, up_buf, dn_buf, y_send, y_got, total, s_buf,
-             rs_sem, ys_sem, z_sem, g_sem, zy_sem, gy_sem, s_sem, own_sem):
+def step_kernel(n, m, part_ref, ls_ref, rs_ref, lr_ref, rr_ref, due_ref,
+                upd_ref, ln_ref, rn_ref, lo_ref, ro_ref,
+                g_ref, zl_ref, zr_ref, lown_ref, rown_ref, t_ref, p_ref, q_ref, w_ref, x_ref,
+                up_buf, dn_buf, y_send, y_got, total, wide_ref, s_buf,
+   rs_sem, ys_sem, zl_sem, zr_sem, g_sem, zly_sem, zry_sem, gy_sem, s_sem):
     outer = n // 2
     rows, cols = total.shape
     me, mp = lax.axis_index("dp"), lax.axis_index("mp")
@@ -23,6 +26,17 @@
     has_up, has_dn = z < outer - 1, z > 0
     peers = [(me, lax.rem(mp + d, m)) for d in range(1, m)]
 
+    bf, f32 = jnp.bfloat16, jnp.float32
+    order = n * rows
+    own = pl.ds(pl.multiple_of(me * rows, rows), rows)
+
+    def is_due(side):
+        return due_ref[side:side + 1, 0:1] == 1
+
+    for side, old, prev, mix, full in ((0, ls_ref, lr_ref, lown_ref, zl_ref), (1, rs_ref, rr_ref, rown_ref, zr_ref)):
+        mix[...] = jnp.where(is_due(side), old[...].astype(bf), prev[...])
+        full[own, :] = mix[...]
+
     barrier = pltpu.get_barrier_semaphore()
 
     def greet(dev):
@@ -52,16 +66,6 @@
         buf, dev = ((up_buf, up), (dn_buf, dn))[way]
         return rc(buf.at[a, h] if src is None else src, buf.at[a, h], rs_sem.at[way, a, h], dev)
 
-    @pl.when(z == 0)
-    def _():
-        for a, h in up_order:
-            rs_copy(0, a, h, mine(a, h)).start()
-
-    @pl.when(z == outer - 1)
-    def _():
-        for a, h in dn_order:
-            rs_copy(1, a, h, mine(a, h)).start()
-
     class Gather:
         def __init__(self, own, full, sem, sem_y):
             self.own, self.full, self.sem, self.sem_y = own, full, sem, sem_y
@@ -86,11 +90,15 @@
         def exists(self, way, step):
             return z - 1 - step >= 0 if way == 0 else z + 1 + step < outer
 
-        def step(self, s):
+        def step(self, s, ends=None):
             for way in (0, 1):
                 block = self.arrival(way, s)
-
-                @pl.when(self.exists(way, s))
+                there = self.exists(way, s)
+                if ends is not None:
+                    at_end = jnp.logical_or(block == 0, block == outer - 1)
+                    there = jnp.logical_and(there, at_end if ends else jnp.logical_not(at_end))
+
+                @pl.when(there)
                 def _():
                     self.line(way, s, block).wait_recv()
                     if s + 1 < outer - 1:
@@ -108,10 +116,21 @@
                     def _():
                         self.across(1 + 2 * s + way, self.arrival(way, s), other).wait()
 
-    zs = Gather(zown_ref, z_ref, z_sem, zy_sem)
-    own_z = pltpu.make_async_copy(zown_ref, at_rows(z_ref, me), own_sem)
-    zs.start()
-    own_z.start()
+    zl = Gather(lown_ref, zl_ref, zl_sem, zly_sem)
+    zr = Gather(rown_ref, zr_ref, zr_sem, zry_sem)
+    zl.start()
+
+    @pl.when(z == 0)
+    def _():
+        for a, h in up_order:
+            rs_copy(0, a, h, mine(a, h)).start()
+
+    @pl.when(z == outer - 1)
+    def _():
+        for a, h in dn_order:
+            rs_copy(1, a, h, mine(a, h)).start()
+
+    zr.start()
 
     def relay(way, a, h):
         rs_copy(way, a, h).wait_recv()
@@ -122,6 +141,8 @@
 
     for k in range(outer - 1):
         a, b = outer - 1 - k, k
+        zl.step(k)
+        zr.step(k, ends=False)
 
         @pl.when(jnp.logical_and(z > 0, z < a))
         def _():
@@ -132,8 +153,6 @@
         def _():
             for h in (0, 1):
                 relay(1, b, h)
-
-        zs.step(k)
 
     def partial_sum(side):
         total[...] = part_ref[pl.ds(pl.multiple_of((2 * z + side) * rows, rows), rows), :].astype(jnp.float32)
@@ -160,6 +179,7 @@
     gs = Gather(own_rows, g_ref, g_sem, gy_sem)
     gs.start()
     for k in range(outer - 1):
+        zr.step(k, ends=True)
         gs.step(k)
     gs.finish()
 
@@ -183,98 +203,130 @@
         for a, h in dn_order:
             pl.when(z > a)(lambda: rs_copy(1, a, h).wait_send())
 
-    own_z.wait()
-    zs.finish()
+    block_sum = jnp.sum(s_buf[0], axis=(0, 1), keepdims=True)
+    gain = (1.0 - decay) / order
+    tile = min(256, order)
+
+    def tiles(body):
+        def one(i, carry):
+            body(pl.ds(pl.multiple_of(i * tile, tile), tile), i)
+            return carry
+
+        lax.fori_loop(0, order // tile, one, 0)
+
+    def diagonal(ref):
+        spot = lax.broadcasted_iota(jnp.int32, (128, 128), 0) == lax.broadcasted_iota(jnp.int32, (128, 128), 1)
+        got = jnp.zeros((128, 128), f32)
+        for i in range(order // 128):
+            block = ref[i * 128:(i + 1) * 128, i * 128:(i + 1) * 128]
+            got += jnp.where(spot, block.astype(f32), 0.0)
+        return jnp.sum(got, axis=(0, 1), keepdims=True)
+
+    def root(side, z_ref, gram):
+        trace = decay * diagonal(z_ref) + gain * block_sum
+        trace = jnp.where(trace > 0.0, trace, 1.0)
+        scale_c = 4.0 * trace / order
+        down = 0.25 / scale_c
+        lift = 0.25 * lax.rsqrt(jnp.sqrt(scale_c))
+
+        def first(at, i):
+            stat = z_ref[at, :].astype(f32) * decay + gram(at) * gain
+            r = lax.broadcasted_iota(jnp.int32, (tile, cols), 0) + i * tile
+            c = lax.broadcasted_iota(jnp.int32, (tile, cols), 1)
+            t_ref[at, :] = (jnp.where(r == c, 1.25, 0.0) - stat * down).astype(bf)
+
+        def second(at, i):
+            p = dot(t_ref[at, :], t_ref[...], ((1,), (0,))).astype(bf)
+            p_ref[at, :] = p
+            w_ref[at, :] = (5.0 * t_ref[at, :].astype(f32) - 4.0 * p.astype(f32)).astype(bf)
+
+        def third(at, i):
+            q_ref[at, :] = dot(p_ref[at, :], p_ref[...], ((1,), (0,))).astype(bf)
+
+        def fourth(at, i):
+            qw = dot(q_ref[at, :], w_ref[...], ((1,), (0,)))
+            new = (lift * (5.0 * t_ref[at, :].astype(f32) - qw)).astype(bf)
+            z_ref[at, :] = jnp.where(is_due(side), new, z_ref[at, :])
+
+        for stage in (first, second, third, fourth):
+            tiles(stage)
+
+    ln_ref[...] = ls_ref[...] * decay + dot(g_ref[own, :], g_ref[...], ((1,), (1,))) * gain
+    wide = wide_ref.shape[0]
+    base = pl.multiple_of(lax.div(me * rows, wide) * wide, wide)
+    wide_ref[...] = dot(g_ref[:, pl.ds(base, wide)].T, g_ref[...], ((1,), (0,)))
+    rn_ref[...] = rs_ref[...] * decay + wide_ref[pl.ds(pl.multiple_of(me * rows - base, rows), rows), :] * gain
+    zl.finish()
+    root(0, zl_ref, lambda at: dot(g_ref[at, :], g_ref[...], ((1,), (1,))))
+    lo_ref[...] = zl_ref[own, :]
+
+    def left_times(at, i):
+        x_ref[at, :] = dot(zl_ref[at, :], g_ref[...], ((1,), (0,))).astype(bf)
+
+    tiles(left_times)
+    zr.finish()
+    root(1, zr_ref, lambda at: dot(g_ref[:, at].T, g_ref[...], ((1,), (0,))))
+    ro_ref[...] = zr_ref[own, :]
     for c in sends:
         c.wait()
-    s_ref[0] = s_buf[0]
-    s_ref[1] = sum(s_buf[d] for d in range(m))
-
-
-def gathered(part, z_own):
+    grand = jnp.sum(sum(s_buf[d] for d in range(m)), axis=(0, 1), keepdims=True)
+    factor = lax.rsqrt(grand / float(m * order * cols) + epsilon)
+
+    def right_times(at, i):
+        upd_ref[at, :] = (dot(x_ref[at, :], zr_ref[...], ((1,), (0,))) * factor).astype(bf)
+
+    tiles(right_times)
+
+
+def dot(a, b, dims):
+    return lax.dot_general(a, b, (dims, ((), ())), preferred_element_type=jnp.float32)
+
+
+def per_device(grad_parts, left_stat, right_stat, left_root, right_root, due):
     n, m = lax.axis_size("dp"), lax.axis_size("mp")
     outer = n // 2
-    order, cols = part.shape
+    order, cols = grad_parts.shape[-2:]
     rows = order // n
     bf, f32 = jnp.bfloat16, jnp.float32
     vm = pl.BlockSpec(memory_space=pltpu.VMEM)
     dma = pltpu.SemaphoreType.DMA
-    return pl.pallas_call(
-        functools.partial(exchange, n, m),
+    flags = jnp.broadcast_to(due[0][:, None], (2, 128))
+    outs = pl.pallas_call(
+        functools.partial(step_kernel, n, m),
         out_shape=(
             jax.ShapeDtypeStruct((order, cols), bf),
-            jax.ShapeDtypeStruct((2, order, cols), bf),
-            jax.ShapeDtypeStruct((2, 8, 128), f32),
+            jax.ShapeDtypeStruct((rows, cols), f32),
+            jax.ShapeDtypeStruct((rows, cols), f32),
+            jax.ShapeDtypeStruct((rows, cols), bf),
+            jax.ShapeDtypeStruct((rows, cols), bf),
         ),
-        in_specs=[vm, vm],
-        out_specs=(vm, vm, vm),
-        scratch_shapes=[
+        in_specs=[vm] * 6,
+        out_specs=(vm,) * 5,
+        scratch_shapes=[pltpu.VMEM((order, cols), bf)] * 3
+        + [pltpu.VMEM((rows, cols), bf)] * 2
+        + [pltpu.VMEM((order, cols), bf)] * 5
+        + [
             pltpu.VMEM((outer, 2, rows, cols), bf),
             pltpu.VMEM((outer, 2, rows, cols), bf),
             pltpu.VMEM((rows, cols), bf),
             pltpu.VMEM((rows, cols), bf),
             pltpu.VMEM((rows, cols), f32),
+            pltpu.VMEM((max(rows, 128), cols), f32),
             pltpu.VMEM((m, 8, 128), f32),
             dma((2, outer, 2, 2)),
             dma((2,)),
             dma((2, outer - 1, 2)),
             dma((2, outer - 1, 2)),
+            dma((2, outer - 1, 2)),
+            dma((2 * outer - 1, 2)),
             dma((2 * outer - 1, 2)),
             dma((2 * outer - 1, 2)),
             dma((m, 2)),
-            dma,
         ],
-        compiler_params=pltpu.CompilerParams(collective_id=0, has_side_effects=True),
-    )(part, z_own)
-
-
-def dot(a, b, dims):
-    return lax.dot_general(a, b, (dims, ((), ())), preferred_element_type=jnp.float32)
-
-
-def root_of(old, prod, square_sum, due):
-    order = old.shape[0]
-    bf, f32 = jnp.bfloat16, jnp.float32
-    gain = (1.0 - decay) / order
-    trace = decay * jnp.trace(old.astype(f32)) + gain * square_sum
-    trace = jnp.where(trace > 0.0, trace, 1.0)
-    scale_c = 4.0 * trace / order
-    eye = jnp.eye(order, dtype=f32)
-    stat = old.astype(f32) * decay + prod * gain
-    t0 = ((5.0 * eye - stat / scale_c) / 4.0).astype(bf)
-    p = dot(t0, t0, ((1,), (0,))).astype(bf)
-    q = dot(p, p, ((1,), (0,))).astype(bf)
-    w = (5.0 * t0.astype(f32) - 4.0 * p.astype(f32)).astype(bf)
-    qw = dot(q, w, ((1,), (0,)))
-    root = (scale_c ** (-0.25) * (5.0 * t0.astype(f32) - qw) / 4.0).astype(bf)
-    return jnp.where(due == 1, root, old)
-
-
-def per_device(grad_parts, left_stat, right_stat, left_root, right_root, due):
-    bf = jnp.bfloat16
-    part = grad_parts[0, 0]
-    rows, order = left_stat.shape[1:]
-    z_own = jnp.stack([
-        jnp.where(due[0, 0] == 1, left_stat[0].astype(bf), left_root[0]),
-        jnp.where(due[0, 1] == 1, right_stat[0].astype(bf), right_root[0]),
-    ])
-    grad, zf, sums = gathered(part, z_own)
-    square_sum, grand_sum = jnp.sum(sums[0]), jnp.sum(sums[1])
-    entry_count = float(lax.axis_size("mp") * order * order)
-    factor = 1.0 / jnp.sqrt(grand_sum / entry_count + epsilon)
-    start = lax.axis_index("dp") * rows
-    gain = (1.0 - decay) / order
-    g_rows = lax.dynamic_slice_in_dim(grad, start, rows, 0)
-    g_cols = lax.dynamic_slice_in_dim(grad, start, rows, 1)
-    left_new = left_stat * decay + dot(g_rows, grad, ((1,), (1,)))[None] * gain
-    right_new = right_stat * decay + dot(g_cols, grad, ((0,), (0,)))[None] * gain
-    left = root_of(zf[0], dot(grad, grad, ((1,), (1,))), square_sum, due[0, 0])
-    right = root_of(zf[1], dot(grad, grad, ((0,), (0,))), square_sum, due[0, 1])
-    x = dot(left, grad, ((1,), (0,))).astype(bf)
-    update = (dot(x, right, ((1,), (0,))) * factor).astype(bf)[None]
-    left_out = lax.dynamic_slice_in_dim(left, start, rows, 0)[None]
-    right_out = lax.dynamic_slice_in_dim(right, start, rows, 0)[None]
-    return (update, left_new, right_new, left_out, right_out)
+        compiler_params=pltpu.CompilerParams(
+            collective_id=0, has_side_effects=True, vmem_limit_bytes=60 * 1024 * 1024),
+    )(grad_parts.reshape(order, cols), left_stat[0], right_stat[0], left_root[0], right_root[0], flags)
+    return tuple(o[None] for o in outs)
 
 
 def solution(mesh):

time: 193 us -> 144 us (0.75)
  matrix products: 49.5 us -> 0 us
  Pallas kernels: 124 us -> 135 us
  other arithmetic: 6.62 us -> 0 us
  between operations: 4.77 us -> 0.66 us
    dot_general x9 -> x0, matrix products: 49.5 us -> none  [dot(): lax.dot_general(a, b, (dims, ((), ())), preferred_element_type=jnp.float32)]
    pallas_call x1, Pallas kernels: 124 us -> 135 us  [per_device(): pl.pallas_call(functools.partial(step_kernel, n, m), out_shape=(jax.Shape...]
    reduce_sum x2 -> x0, other arithmetic: 4.41 us -> none  [the longest x1 3.12 us: root_of(): trace = decay * jnp.trace(old.astype(f32)) + gain * square_sum]
    unnamed x10 -> x13, local copies, waits for them, and re-layouts: 2.69 us -> 6.17 us
    broadcast_in_dim x2 -> x1, local copies, waits for them, and re-layouts: 3.34 us -> 1.29 us  [per_device(): flags = jnp.broadcast_to(due[0][:, None], (2, 128))]
where the time goes in v2:
time: 144 us; the launch traced here: 143 us
  Pallas kernels  135 us (94%)
  local copies, waits for them, and re-layouts  7.46 us (5%)
    pallas_call x1, Pallas kernels, per_device(): pl.pallas_call(functools.partial(step_kernel, n, m), out_shape=(jax.Shape...  135 us
    unnamed x13, local copies, waits for them, and re-layouts  6.17 us

profile of v2, /device:TPU:0, one launch (start us, length us, event | category | flops | bytes accessed | tf_op | source)
XLA Modules:
  0.0 143.4 jit_solution(12374543482827786106)
XLA Ops:
  0.6 1.3 broadcast_in_dim.23.due_ref
  1.9 135.3 %shard_map.101 = (bf16[1024,1024]{1,0:T(8,128)(2,1)}, f32[128,1024]{1,0:T(8,128)}, f32[128,1024]{1,0:T(8,128)}, bf16[128,1024]{1,0:T(8,128)(2,1)}, bf16[128,1024]{1,0:T(8,128)(2,1)}) custom-call(bf16[1024,1024]{1,0:T(8,128)(2,1)} %bitcast.11, f32[128,1024]{1,0:T(8,128)} %bitcast.15, f32[128,1024]{1,0:T(8,128)} %bitcast.16, bf16[128,1024]{1,0:T(8,128)(2,1)} %bitcast.19, ...), custom_call_target="tpu_custom_call" | custom-call | tf_op jit(solution)/shard_map/pallas_call | solution.py:294
  137.2 0.0 copy-start.1
  137.3 0.0 copy-start
  137.3 3.2 %copy.16 = bf16[1,1024,1024]{2,1,0:T(8,128)(2,1)} copy(bf16[1,1024,1024]{2,1,0:T(8,128)(2,1)} %bitcast.12) | data formatting | bytes 4194304
  140.4 0.0 copy-done.1
  140.4 0.0 copy-start.3
  140.4 0.0 copy-start.2
  140.4 0.8 copy.17
  141.2 0.0 copy-done
  141.2 0.8 copy.18
  142.0 0.0 copy-done.3
  142.0 0.7 copy.19
  142.7 0.0 copy-done.2
  142.7 0.7 copy.20
Async XLA Ops:
  137.2 3.2 %copy-start.1 = (f32[128,1024]{1,0:T(8,128)S(1)}, f32[128,1024]{1,0:T(8,128)}, u32[]{:S(2)}) copy-start(f32[128,1024]{1,0:T(8,128)} %get-tuple-element.11) | copy-start | bytes 1572868
  137.3 4.0 %copy-start = (f32[128,1024]{1,0:T(8,128)S(1)}, f32[128,1024]{1,0:T(8,128)}, u32[]{:S(2)}) copy-start(f32[128,1024]{1,0:T(8,128)} %get-tuple-element.12) | copy-start | bytes 1572868
  140.4 1.6 %copy-start.3 = (bf16[128,1024]{1,0:T(8,128)(2,1)S(1)}, bf16[128,1024]{1,0:T(8,128)(2,1)}, u32[]{:S(2)}) copy-start(bf16[128,1024]{1,0:T(8,128)(2,1)} %get-tuple-element.13) | copy-start | bytes 786436
  140.4 2.3 %copy-start.2 = (bf16[128,1024]{1,0:T(8,128)(2,1)S(1)}, bf16[128,1024]{1,0:T(8,128)(2,1)}, u32[]{:S(2)}) copy-start(bf16[128,1024]{1,0:T(8,128)(2,1)} %get-tuple-element.14) | copy-start | bytes 786436

commit v3 on v2

--- a/solution.py
+++ b/solution.py
@@ -15,8 +15,8 @@
 def step_kernel(n, m, part_ref, ls_ref, rs_ref, lr_ref, rr_ref, due_ref,
                 upd_ref, ln_ref, rn_ref, lo_ref, ro_ref,
                 g_ref, zl_ref, zr_ref, lown_ref, rown_ref, t_ref, p_ref, q_ref, w_ref, x_ref,
-                up_buf, dn_buf, y_send, y_got, total, wide_ref, s_buf,
-   rs_sem, ys_sem, zl_sem, zr_sem, g_sem, zly_sem, zry_sem, gy_sem, s_sem):
+                up_buf, dn_buf, y_got, total, wide_ref, s_buf,
+   rs_sem, ys_sem, zl_sem, zr_sem, zp_sem, g_sem, zly_sem, zry_sem, gy_sem, s_sem):
     outer = n // 2
     rows, cols = total.shape
     me, mp = lax.axis_index("dp"), lax.axis_index("mp")
@@ -31,7 +31,7 @@
     own = pl.ds(pl.multiple_of(me * rows, rows), rows)
 
     def is_due(side):
-        return due_ref[side:side + 1, 0:1] == 1
+        return due_ref[0:1, side:side + 1] == 1
 
     for side, old, prev, mix, full in ((0, ls_ref, lr_ref, lown_ref, zl_ref), (1, rs_ref, rr_ref, rown_ref, zr_ref)):
         mix[...] = jnp.where(is_due(side), old[...].astype(bf), prev[...])
@@ -57,22 +57,27 @@
         return ref.at[..., pl.ds(pl.multiple_of(block * rows, rows), rows), :]
 
     def mine(a, h):
-        return part_ref.at[pl.ds((2 * a + h) * rows, rows), :]
-
-    up_order = [(a, h) for a in range(outer - 1, 0, -1) for h in (0, 1)]
-    dn_order = [(a, h) for a in range(outer - 1) for h in (0, 1)]
-
-    def rs_copy(way, a, h, src=None):
+        return at_rows(part_ref, 2 * a + h)
+
+    def rs_copy(way, a):
         buf, dev = ((up_buf, up), (dn_buf, dn))[way]
-        return rc(buf.at[a, h] if src is None else src, buf.at[a, h], rs_sem.at[way, a, h], dev)
+        return rc(buf.at[a], buf.at[a], rs_sem.at[way, a], dev)
+
+    def pair_copy(a, side):
+        return rc(mine(a, side), y_got.at[a], ys_sem.at[a], pair)
+
+    def by_distance(body):
+        for d in range(outer - 1, 0, -1):
+            pl.when(z + d < outer)(lambda: body(0, z + d))
+            pl.when(z - d >= 0)(lambda: body(1, z - d))
 
     class Gather:
-        def __init__(self, own, full, sem, sem_y):
-            self.own, self.full, self.sem, self.sem_y = own, full, sem, sem_y
+        def __init__(self, own, full, sem, sem_y, side):
+            self.own, self.full, self.sem, self.sem_y, self.side = own, full, sem, sem_y, side
 
         def line(self, way, step, block):
             dev = (up, dn)[way]
-            where = at_rows(self.full, 2 * block + y)
+            where = at_rows(self.full, 2 * block + self.side)
             return rc(self.own if step == 0 else where, where, self.sem.at[way, step], dev)
 
         def across(self, index, block, side):
@@ -82,7 +87,8 @@
         def start(self):
             pl.when(has_up)(lambda: self.line(0, 0, z).start())
             pl.when(has_dn)(lambda: self.line(1, 0, z).start())
-            self.across(0, z, y).start()
+            if self.sem_y is not None:
+                self.across(0, z, y).start()
 
         def arrival(self, way, step):
             return z - 1 - step if way == 0 else z + 1 + step
@@ -90,96 +96,80 @@
         def exists(self, way, step):
             return z - 1 - step >= 0 if way == 0 else z + 1 + step < outer
 
-        def step(self, s, ends=None):
+        def step(self, s):
             for way in (0, 1):
                 block = self.arrival(way, s)
-                there = self.exists(way, s)
-                if ends is not None:
-                    at_end = jnp.logical_or(block == 0, block == outer - 1)
-                    there = jnp.logical_and(there, at_end if ends else jnp.logical_not(at_end))
-
-                @pl.when(there)
+
+                @pl.when(self.exists(way, s))
                 def _():
                     self.line(way, s, block).wait_recv()
                     if s + 1 < outer - 1:
                         pl.when((has_up, has_dn)[way])(lambda: self.line(way, s + 1, block).start())
-                    self.across(1 + 2 * s + way, block, y).start()
+                    if self.sem_y is not None:
+                        self.across(1 + 2 * s + way, block, y).start()
 
         def finish(self):
-            self.across(0, z, other).wait()
+            if self.sem_y is not None:
+                self.across(0, z, other).wait()
             for s in range(outer - 1):
                 for way in (0, 1):
                     sent = jnp.logical_and((z - s >= 0, z + s < outer)[way], (has_up, has_dn)[way])
                     pl.when(sent)(lambda: self.line(way, s, z).wait_send())
 
-                    @pl.when(self.exists(way, s))
-                    def _():
-                        self.across(1 + 2 * s + way, self.arrival(way, s), other).wait()
-
-    zl = Gather(lown_ref, zl_ref, zl_sem, zly_sem)
-    zr = Gather(rown_ref, zr_ref, zr_sem, zry_sem)
+                    if self.sem_y is not None:
+                        index, block = 1 + 2 * s + way, self.arrival(way, s)
+                        pl.when(self.exists(way, s))(lambda: self.across(index, block, other).wait())
+
+    own_rows = at_rows(g_ref, me)
+    zl = Gather(lown_ref, zl_ref, zl_sem, zly_sem, y)
+    zr = Gather(rown_ref, zr_ref, zr_sem, None, y)
+    zp = Gather(at_rows(zr_ref, 2 * z + other), zr_ref, zp_sem, None, other)
+    gs = Gather(own_rows, g_ref, g_sem, gy_sem, y)
+
+    def swap(side):
+        return rc(rown_ref, at_rows(zr_ref, 2 * z + side), zry_sem, pair)
+
+    by_distance(lambda way, a: pair_copy(a, other).start())
+    pair_copy(z, other).start()
     zl.start()
-
-    @pl.when(z == 0)
-    def _():
-        for a, h in up_order:
-            rs_copy(0, a, h, mine(a, h)).start()
-
-    @pl.when(z == outer - 1)
-    def _():
-        for a, h in dn_order:
-            rs_copy(1, a, h, mine(a, h)).start()
-
+    swap(y).start()
     zr.start()
 
-    def relay(way, a, h):
-        rs_copy(way, a, h).wait_recv()
+    def f32_of(ref):
+        return ref[...].astype(f32)
+
+    def relay(way, a):
+        pair_copy(a, y).wait_recv()
         buf = (up_buf, dn_buf)[way]
-        both = buf[a, h].astype(jnp.float32) + mine(a, h)[...].astype(jnp.float32)
-        buf[a, h] = both.astype(jnp.bfloat16)
-        rs_copy(way, a, h).start()
-
+        total[...] = f32_of(mine(a, y)) + f32_of(y_got.at[a])
+
+        @pl.when((has_dn, has_up)[way])
+        def _():
+            rs_copy(way, a).wait_recv()
+            total[...] += f32_of(buf.at[a])
+
+        buf[a] = total[...].astype(bf)
+        rs_copy(way, a).start()
+
+    for d in range(outer - 1, 0, -1):
+        pl.when(z + d < outer)(lambda: relay(0, z + d))
+        pl.when(z - d >= 0)(lambda: relay(1, z - d))
+        zl.step(outer - 1 - d)
+
+    pair_copy(z, y).wait_recv()
+    total[...] = f32_of(mine(z, y)) + f32_of(y_got.at[z])
+    for way in (0, 1):
+        @pl.when((has_dn, has_up)[way])
+        def _():
+            rs_copy(way, z).wait_recv()
+            total[...] += f32_of((up_buf, dn_buf)[way].at[z])
+
+    own_rows[...] = total[...].astype(bf)
+    gs.start()
+    swap(other).wait()
+    zp.start()
     for k in range(outer - 1):
-        a, b = outer - 1 - k, k
-        zl.step(k)
-        zr.step(k, ends=False)
-
-        @pl.when(jnp.logical_and(z > 0, z < a))
-        def _():
-            for h in (0, 1):
-                relay(0, a, h)
-
-        @pl.when(jnp.logical_and(z < outer - 1, z > b))
-        def _():
-            for h in (0, 1):
-                relay(1, b, h)
-
-    def partial_sum(side):
-        total[...] = part_ref[pl.ds(pl.multiple_of((2 * z + side) * rows, rows), rows), :].astype(jnp.float32)
-
-        @pl.when(has_dn)
-        def _():
-            rs_copy(0, z, side).wait_recv()
-            total[...] += up_buf[z, side].astype(jnp.float32)
-
-        @pl.when(has_up)
-        def _():
-            rs_copy(1, z, side).wait_recv()
-            total[...] += dn_buf[z, side].astype(jnp.float32)
-
-    partial_sum(other)
-    y_send[...] = total[...].astype(jnp.bfloat16)
-    cross = rc(y_send, y_got, ys_sem, pair)
-    cross.start()
-    partial_sum(y)
-    cross.wait()
-    own_rows = at_rows(g_ref, me)
-    own_rows[...] = (total[...] + y_got[...].astype(jnp.float32)).astype(jnp.bfloat16)
-
-    gs = Gather(own_rows, g_ref, g_sem, gy_sem)
-    gs.start()
-    for k in range(outer - 1):
-        zr.step(k, ends=True)
+        zr.step(k)
         gs.step(k)
     gs.finish()
 
@@ -193,16 +183,9 @@
     for c in sends:
         c.start()
 
-    @pl.when(has_up)
-    def _():
-        for a, h in up_order:
-            pl.when(z < a)(lambda: rs_copy(0, a, h).wait_send())
-
-    @pl.when(has_dn)
-    def _():
-        for a, h in dn_order:
-            pl.when(z > a)(lambda: rs_copy(1, a, h).wait_send())
-
+    by_distance(lambda way, a: rs_copy(way, a).wait_send())
+    by_distance(lambda way, a: pair_copy(a, other).wait_send())
+    pair_copy(z, other).wait_send()
     block_sum = jnp.sum(s_buf[0], axis=(0, 1), keepdims=True)
     gain = (1.0 - decay) / order
     tile = min(256, order)
@@ -251,11 +234,14 @@
         for stage in (first, second, third, fourth):
             tiles(stage)
 
+    zp.step(0)
     ln_ref[...] = ls_ref[...] * decay + dot(g_ref[own, :], g_ref[...], ((1,), (1,))) * gain
     wide = wide_ref.shape[0]
     base = pl.multiple_of(lax.div(me * rows, wide) * wide, wide)
     wide_ref[...] = dot(g_ref[:, pl.ds(base, wide)].T, g_ref[...], ((1,), (0,)))
     rn_ref[...] = rs_ref[...] * decay + wide_ref[pl.ds(pl.multiple_of(me * rows - base, rows), rows), :] * gain
+    for k in range(1, outer - 1):
+        zp.step(k)
     zl.finish()
     root(0, zl_ref, lambda at: dot(g_ref[at, :], g_ref[...], ((1,), (1,))))
     lo_ref[...] = zl_ref[own, :]
@@ -265,6 +251,7 @@
 
     tiles(left_times)
     zr.finish()
+    zp.finish()
     root(1, zr_ref, lambda at: dot(g_ref[:, at].T, g_ref[...], ((1,), (0,))))
     ro_ref[...] = zr_ref[own, :]
     for c in sends:
@@ -290,7 +277,6 @@
     bf, f32 = jnp.bfloat16, jnp.float32
     vm = pl.BlockSpec(memory_space=pltpu.VMEM)
     dma = pltpu.SemaphoreType.DMA
-    flags = jnp.broadcast_to(due[0][:, None], (2, 128))
     outs = pl.pallas_call(
         functools.partial(step_kernel, n, m),
         out_shape=(
@@ -306,26 +292,26 @@
         + [pltpu.VMEM((rows, cols), bf)] * 2
         + [pltpu.VMEM((order, cols), bf)] * 5
         + [
-            pltpu.VMEM((outer, 2, rows, cols), bf),
-            pltpu.VMEM((outer, 2, rows, cols), bf),
-            pltpu.VMEM((rows, cols), bf),
-            pltpu.VMEM((rows, cols), bf),
+            pltpu.VMEM((outer, rows, cols), bf),
+            pltpu.VMEM((outer, rows, cols), bf),
+            pltpu.VMEM((outer, rows, cols), bf),
             pltpu.VMEM((rows, cols), f32),
             pltpu.VMEM((max(rows, 128), cols), f32),
             pltpu.VMEM((m, 8, 128), f32),
-            dma((2, outer, 2, 2)),
-            dma((2,)),
+            dma((2, outer, 2)),
+            dma((outer, 2)),
+            dma((2, outer - 1, 2)),
             dma((2, outer - 1, 2)),
             dma((2, outer - 1, 2)),
             dma((2, outer - 1, 2)),
             dma((2 * outer - 1, 2)),
-            dma((2 * outer - 1, 2)),
+            dma((2,)),
             dma((2 * outer - 1, 2)),
             dma((m, 2)),
         ],
         compiler_params=pltpu.CompilerParams(
             collective_id=0, has_side_effects=True, vmem_limit_bytes=60 * 1024 * 1024),
-    )(grad_parts.reshape(order, cols), left_stat[0], right_stat[0], left_root[0], right_root[0], flags)
+    )(grad_parts.reshape(order, cols), left_stat[0], right_stat[0], left_root[0], right_root[0], due)
     return tuple(o[None] for o in outs)
 
 

time: 144 us -> 136 us (0.944)
  Pallas kernels: 135 us -> 129 us
    pallas_call x1, Pallas kernels: 135 us -> 129 us  [per_device(): pl.pallas_call(functools.partial(step_kernel, n, m), out_shape=(jax.Shape...]
where the time goes in v3:
time: 136 us
  Pallas kernels  129 us (95%)
  local copies, waits for them, and re-layouts  6.17 us (5%)
    pallas_call x1, Pallas kernels, per_device(): pl.pallas_call(functools.partial(step_kernel, n, m), out_shape=(jax.Shape...  129 us
    unnamed x13, local copies, waits for them, and re-layouts  6.17 us

profile of v3, /device:TPU:0, one launch (start us, length us, event | category | flops | bytes accessed | tf_op | source)
XLA Modules:
  0.0 136.1 jit_solution(16328677930658992036)
XLA Ops:
  0.6 129.3 %shard_map.101 = (bf16[1024,1024]{1,0:T(8,128)(2,1)}, f32[128,1024]{1,0:T(8,128)}, f32[128,1024]{1,0:T(8,128)}, bf16[128,1024]{1,0:T(8,128)(2,1)}, bf16[128,1024]{1,0:T(8,128)(2,1)}) custom-call(bf16[1024,1024]{1,0:T(8,128)(2,1)} %bitcast.10, f32[128,1024]{1,0:T(8,128)} %bitcast.14, f32[128,1024]{1,0:T(8,128)} %bitcast.15, bf16[128,1024]{1,0:T(8,128)(2,1)} %bitcast.18, ...), custom_call_target="tpu_custom_call" | custom-call | tf_op jit(solution)/shard_map/pallas_call | solution.py:280
  129.9 0.0 copy-start.1
  129.9 0.0 copy-start
  129.9 3.2 %copy.16 = bf16[1,1024,1024]{2,1,0:T(8,128)(2,1)} copy(bf16[1,1024,1024]{2,1,0:T(8,128)(2,1)} %bitcast.11) | data formatting | bytes 4194304
  133.1 0.0 copy-done.1
  133.1 0.0 copy-start.3
  133.1 0.0 copy-start.2
  133.1 0.8 copy.17
  133.9 0.0 copy-done
  133.9 0.8 copy.18
  134.7 0.0 copy-done.3
  134.7 0.7 copy.19
  135.4 0.0 copy-done.2
  135.4 0.7 copy.20
Async XLA Ops:
  129.9 3.2 %copy-start.1 = (f32[128,1024]{1,0:T(8,128)S(1)}, f32[128,1024]{1,0:T(8,128)}, u32[]{:S(2)}) copy-start(f32[128,1024]{1,0:T(8,128)} %get-tuple-element.11) | copy-start | bytes 1572868
  129.9 4.0 %copy-start = (f32[128,1024]{1,0:T(8,128)S(1)}, f32[128,1024]{1,0:T(8,128)}, u32[]{:S(2)}) copy-start(f32[128,1024]{1,0:T(8,128)} %get-tuple-element.12) | copy-start | bytes 1572868
  133.1 1.6 %copy-start.3 = (bf16[128,1024]{1,0:T(8,128)(2,1)S(1)}, bf16[128,1024]{1,0:T(8,128)(2,1)}, u32[]{:S(2)}) copy-start(bf16[128,1024]{1,0:T(8,128)(2,1)} %get-tuple-element.13) | copy-start | bytes 786436
  133.1 2.3 %copy-start.2 = (bf16[128,1024]{1,0:T(8,128)(2,1)S(1)}, bf16[128,1024]{1,0:T(8,128)(2,1)}, u32[]{:S(2)}) copy-start(bf16[128,1024]{1,0:T(8,128)(2,1)} %get-tuple-element.14) | copy-start | bytes 786436

commit v4 on v3

--- a/solution.py
+++ b/solution.py
@@ -133,7 +133,6 @@
     pair_copy(z, other).start()
     zl.start()
     swap(y).start()
-    zr.start()
 
     def f32_of(ref):
         return ref[...].astype(f32)
@@ -166,11 +165,18 @@
 
     own_rows[...] = total[...].astype(bf)
     gs.start()
+    zr.start()
     swap(other).wait()
     zp.start()
+
+    def late(*steps):
+        for k in steps:
+            zr.step(k)
+            zp.step(k)
+
     for k in range(outer - 1):
-        zr.step(k)
         gs.step(k)
+    late(0)
     gs.finish()
 
     def square(i, acc):
@@ -205,7 +211,7 @@
             got += jnp.where(spot, block.astype(f32), 0.0)
         return jnp.sum(got, axis=(0, 1), keepdims=True)
 
-    def root(side, z_ref, gram):
+    def root(side, z_ref, gram, between):
         trace = decay * diagonal(z_ref) + gain * block_sum
         trace = jnp.where(trace > 0.0, trace, 1.0)
         scale_c = 4.0 * trace / order
@@ -231,19 +237,24 @@
             new = (lift * (5.0 * t_ref[at, :].astype(f32) - qw)).astype(bf)
             z_ref[at, :] = jnp.where(is_due(side), new, z_ref[at, :])
 
-        for stage in (first, second, third, fourth):
+        for k, stage in enumerate((first, second, third, fourth)):
             tiles(stage)
-
-    zp.step(0)
+            between(k)
+
     ln_ref[...] = ls_ref[...] * decay + dot(g_ref[own, :], g_ref[...], ((1,), (1,))) * gain
     wide = wide_ref.shape[0]
     base = pl.multiple_of(lax.div(me * rows, wide) * wide, wide)
     wide_ref[...] = dot(g_ref[:, pl.ds(base, wide)].T, g_ref[...], ((1,), (0,)))
     rn_ref[...] = rs_ref[...] * decay + wide_ref[pl.ds(pl.multiple_of(me * rows - base, rows), rows), :] * gain
-    for k in range(1, outer - 1):
-        zp.step(k)
     zl.finish()
-    root(0, zl_ref, lambda at: dot(g_ref[at, :], g_ref[...], ((1,), (1,))))
+
+    def relay_late(k):
+        if k == 0:
+            late(*range(1, min(2, outer - 1)))
+        if k == 1:
+            late(*range(2, outer - 1))
+
+    root(0, zl_ref, lambda at: dot(g_ref[at, :], g_ref[...], ((1,), (1,))), relay_late)
     lo_ref[...] = zl_ref[own, :]
 
     def left_times(at, i):
@@ -252,7 +263,7 @@
     tiles(left_times)
     zr.finish()
     zp.finish()
-    root(1, zr_ref, lambda at: dot(g_ref[:, at].T, g_ref[...], ((1,), (0,))))
+    root(1, zr_ref, lambda at: dot(g_ref[:, at].T, g_ref[...], ((1,), (0,))), lambda k: None)
     ro_ref[...] = zr_ref[own, :]
     for c in sends:
         c.wait()

time: 136 us -> 133 us (0.978)
  Pallas kernels: 129 us -> 126 us
    pallas_call x1, Pallas kernels: 129 us -> 126 us  [per_device(): pl.pallas_call(functools.partial(step_kernel, n, m), out_shape=(jax.Shape...]
where the time goes in v4:
time: 133 us
  Pallas kernels  126 us (95%)
  local copies, waits for them, and re-layouts  6.17 us (5%)
    pallas_call x1, Pallas kernels, per_device(): pl.pallas_call(functools.partial(step_kernel, n, m), out_shape=(jax.Shape...  126 us
    unnamed x13, local copies, waits for them, and re-layouts  6.17 us

profile of v4, /device:TPU:0, one launch (start us, length us, event | category | flops | bytes accessed | tf_op | source)
XLA Modules:
  0.0 132.8 jit_solution(11006438082674034041)
XLA Ops:
  0.6 126.0 %shard_map.101 = (bf16[1024,1024]{1,0:T(8,128)(2,1)}, f32[128,1024]{1,0:T(8,128)}, f32[128,1024]{1,0:T(8,128)}, bf16[128,1024]{1,0:T(8,128)(2,1)}, bf16[128,1024]{1,0:T(8,128)(2,1)}) custom-call(bf16[1024,1024]{1,0:T(8,128)(2,1)} %bitcast.10, f32[128,1024]{1,0:T(8,128)} %bitcast.14, f32[128,1024]{1,0:T(8,128)} %bitcast.15, bf16[128,1024]{1,0:T(8,128)(2,1)} %bitcast.18, ...), custom_call_target="tpu_custom_call" | custom-call | tf_op jit(solution)/shard_map/pallas_call | solution.py:291
  126.6 0.0 copy-start.1
  126.7 0.0 copy-start
  126.7 3.2 %copy.16 = bf16[1,1024,1024]{2,1,0:T(8,128)(2,1)} copy(bf16[1,1024,1024]{2,1,0:T(8,128)(2,1)} %bitcast.11) | data formatting | bytes 4194304
  129.8 0.0 copy-done.1
  129.8 0.0 copy-start.3
  129.8 0.0 copy-start.2
  129.8 0.8 copy.17
  130.6 0.0 copy-done
  130.6 0.8 copy.18
  131.4 0.0 copy-done.3
  131.4 0.7 copy.19
  132.1 0.0 copy-done.2
  132.1 0.7 copy.20
Async XLA Ops:
  126.6 3.2 %copy-start.1 = (f32[128,1024]{1,0:T(8,128)S(1)}, f32[128,1024]{1,0:T(8,128)}, u32[]{:S(2)}) copy-start(f32[128,1024]{1,0:T(8,128)} %get-tuple-element.11) | copy-start | bytes 1572868
  126.7 4.0 %copy-start = (f32[128,1024]{1,0:T(8,128)S(1)}, f32[128,1024]{1,0:T(8,128)}, u32[]{:S(2)}) copy-start(f32[128,1024]{1,0:T(8,128)} %get-tuple-element.12) | copy-start | bytes 1572868
  129.8 1.6 %copy-start.3 = (bf16[128,1024]{1,0:T(8,128)(2,1)S(1)}, bf16[128,1024]{1,0:T(8,128)(2,1)}, u32[]{:S(2)}) copy-start(bf16[128,1024]{1,0:T(8,128)(2,1)} %get-tuple-element.13) | copy-start | bytes 786436
  129.8 2.3 %copy-start.2 = (bf16[128,1024]{1,0:T(8,128)(2,1)S(1)}, bf16[128,1024]{1,0:T(8,128)(2,1)}, u32[]{:S(2)}) copy-start(bf16[128,1024]{1,0:T(8,128)(2,1)} %get-tuple-element.14) | copy-start | bytes 786436
